TPU v7x, 256 devices: a whole 4x4x8 slice. The times are simulated.
256 devices in a mesh: section: 16 (over y_hi, x, core), ray: 8 (over z), dp: 2 (over y_lo).
Axes of the slice: x: 4, y: 4 (y_hi: 2, y_lo: 2; y = y_hi * 2 + y_lo), z: 8, core: 2. Of those that a mesh axis runs over, the one named last changes fastest.
Arguments:
- section_tokens: bfloat16 [16, 2, 1024, 1024], P('section', 'dp', 'ray'), may hold values from -6 to 6
- enc_ln1: float32 [16, 1024], P('section'), may hold values from 0.5 to 1.5
- enc_qkv: bfloat16 [16, 1024, 3, 1024], P('section', None, None, 'ray'), may hold values from -40 to 40
- enc_out: bfloat16 [16, 1024, 1024], P('section', 'ray'), may hold values from -0.1875 to 0.1875
- enc_ln2: float32 [16, 1024], P('section'), may hold values from 0.5 to 1.5
- enc_up: bfloat16 [16, 1024, 4096], P('section', None, 'ray'), may hold values from -0.1875 to 0.1875
- enc_down: bfloat16 [16, 4096, 1024], P('section', 'ray'), may hold values from -0.09375 to 0.09375
- set_latent: bfloat16 [2, 1024, 1024], P('dp', 'ray'), may hold values from -6 to 6
- ray_queries: bfloat16 [2, 32768, 1024], P('dp', ('section', 'ray')), may hold values from -6 to 6
- dec_query: bfloat16 [1024, 1024], P('section'), may hold values from -40 to 40
- dec_kv: bfloat16 [1024, 2, 1024], P('section'), may hold values from -1 to 1
- dec_out: bfloat16 [1024, 1024], P('section'), may hold values from -0.1875 to 0.1875
- feature_grad: bfloat16 [2, 32768, 1024], P('dp', ('section', 'ray')), may hold values from -2 to 2
Outputs:
- handed: bfloat16 [16, 2, 1024, 1024], P('section', 'dp', 'ray')
- finished: bfloat16 [2, 1024, 1024], P('dp', 'ray', 'section')
- ray_features: bfloat16 [2, 32768, 1024], P('dp', ('section', 'ray'))
- latent_grad: bfloat16 [2, 1024, 1024], P('dp', 'ray')
- out_grad: float32 [1024, 1024], replicated
All inputs are finite; a program needn't handle non-finite values.
Results may differ from a plain program's by a relative error of at most 0.022.
The roundings to bfloat16 on the way count: a program that leaves them out, or rounds other values in their place, can miss the bound.
Values may be sent and summed in bfloat16 or wider, within the bound.
No kernel may reach another device: no remote copies, remote signals or barrier semaphores. Data moves between devices by JAX's collectives and lax.ppermute only.
A program may use at most 128 MiB of HBM per device.

v0:
```python
import math
import jax
import jax.numpy as jnp
from jax import lax
from jax.sharding import PartitionSpec as P

HEADS = 16


def shifted(value, axis, by):
    count = lax.axis_size(axis)
    pairs = [(i, i + by) for i in range(count) if 0 <= i + by < count]
    return lax.ppermute(value, axis, pairs)


def spread_2(value, axis, root):
    mine = lax.axis_index(axis) == root
    return lax.psum(jnp.where(mine, value, jnp.zeros_like(value)), axis)


def layer_norm(values, gain):
    values = values.astype(jnp.float32)
    center = values - jnp.mean(values, -1, keepdims=True)
    spread = jnp.mean(center * center, -1, keepdims=True)
    return center * lax.rsqrt(spread + 1e-05) * gain


def softmax_rows(scores):
    top = jnp.max(scores, -1, keepdims=True)
    expo = jnp.exp(scores - top)
    return expo / jnp.sum(expo, -1, keepdims=True)


def attend_heads(packed, head_dim):
    length = packed.shape[0]
    heads = packed.shape[1] // (3 * head_dim)
    split = packed.reshape(length, 3, heads, head_dim)
    scores = jnp.einsum(
        "qhd,khd->hqk", split[:, 0], split[:, 1], preferred_element_type=jnp.float32
    ) / math.sqrt(head_dim)
    probs = softmax_rows(scores).astype(jnp.bfloat16)
    mixed = jnp.einsum("hqk,khd->qhd", probs, split[:, 2], preferred_element_type=jnp.float32)
    return mixed.astype(jnp.bfloat16).reshape(length, heads * head_dim)


def latent_rows(pair_sum, w_pairs):
    result = lax.dot_general(
        pair_sum[:, 0],
        w_pairs[:, 0, :],
        (((1,), (1,)), ((), ())),
        preferred_element_type=jnp.float32,
    )
    result = result + lax.dot_general(
        pair_sum[:, 1],
        w_pairs[:, 1, :],
        (((1,), (1,)), ((), ())),
        preferred_element_type=jnp.float32,
    )
    return result.astype(jnp.bfloat16)


def local(
    section_tokens,
    enc_ln1,
    enc_qkv,
    enc_out,
    enc_ln2,
    enc_up,
    enc_down,
    set_latent,
    ray_queries,
    dec_query,
    dec_kv,
    dec_out,
    feature_grad,
):
    tokens = section_tokens[0, 0]
    width = tokens.shape[1]
    head_dim = width // HEADS
    local_width = enc_out.shape[1]
    w_qkv = enc_qkv[0].reshape(width, 3 * local_width)
    w_attn_out = enc_out[0]
    w_upper = enc_up[0]
    w_lower = enc_down[0]
    gain_one = enc_ln1[0]
    gain_two = enc_ln2[0]
    normed = layer_norm(tokens, gain_one).astype(jnp.bfloat16)
    packed = jnp.dot(
        lax.all_gather(normed, "ray", axis=0, tiled=True), w_qkv, preferred_element_type=jnp.float32
    ).astype(jnp.bfloat16)
    mixed = attend_heads(packed, head_dim)
    attn_rows = lax.psum_scatter(
        jnp.dot(mixed, w_attn_out, preferred_element_type=jnp.float32).astype(jnp.bfloat16),
        "ray",
        scatter_dimension=0,
        tiled=True,
    ).astype(jnp.float32)
    hidden = (tokens.astype(jnp.float32) + attn_rows).astype(jnp.bfloat16)
    upper = jax.nn.gelu(
        jnp.dot(
            lax.all_gather(
                layer_norm(hidden, gain_two).astype(jnp.bfloat16), "ray", axis=0, tiled=True
            ),
            w_upper,
            preferred_element_type=jnp.float32,
        ),
        approximate=True,
    ).astype(jnp.bfloat16)
    lower_rows = lax.psum_scatter(
        jnp.dot(upper, w_lower, preferred_element_type=jnp.float32).astype(jnp.bfloat16),
        "ray",
        scatter_dimension=0,
        tiled=True,
    ).astype(jnp.float32)
    layer_out = (hidden.astype(jnp.float32) + lower_rows).astype(jnp.bfloat16)
    handed = shifted(layer_out, "section", 1)
    finished_all = spread_2(layer_out, "section", lax.axis_size("section") - 1)
    columns = width // lax.axis_size("section")
    finished = lax.dynamic_slice_in_dim(
        finished_all, lax.axis_index("section") * columns, columns, 1
    )
    w_query, w_pairs, w_mix = (
        lax.all_gather(dec_query, "section", axis=0, tiled=True),
        lax.all_gather(dec_kv, "section", axis=0, tiled=True),
        lax.all_gather(dec_out, "section", axis=0, tiled=True),
    )
    latent = set_latent[0]
    queries = ray_queries[0]
    cotangent = feature_grad[0]
    flat_pairs = w_pairs.reshape(width, 2 * width)
    key_values = lax.all_gather(
        jnp.dot(latent, flat_pairs, preferred_element_type=jnp.float32).astype(jnp.bfloat16),
        "ray",
        axis=0,
        tiled=True,
    )
    scene_len = key_values.shape[0]
    ray_rows = queries.shape[0]
    scale = 1.0 / math.sqrt(head_dim)
    keys = key_values[:, :width].reshape(scene_len, HEADS, head_dim)
    values = key_values[:, width:].reshape(scene_len, HEADS, head_dim)
    query = (
        jnp.dot(queries, w_query, preferred_element_type=jnp.float32)
        .astype(jnp.bfloat16)
        .reshape(ray_rows, HEADS, head_dim)
    )
    scores = jnp.einsum("rhd,lhd->hrl", query, keys, preferred_element_type=jnp.float32) * scale
    probs = softmax_rows(scores)
    probs_low = probs.astype(jnp.bfloat16)
    attended = (
        jnp.einsum("hrl,lhd->rhd", probs_low, values, preferred_element_type=jnp.float32)
        .astype(jnp.bfloat16)
        .reshape(ray_rows, width)
    )
    features = (
        queries.astype(jnp.float32) + jnp.dot(attended, w_mix, preferred_element_type=jnp.float32)
    ).astype(jnp.bfloat16)
    mix_term = lax.dot_general(
        attended, cotangent, (((0,), (0,)), ((), ())), preferred_element_type=jnp.float32
    )
    out_grad = lax.psum(mix_term, ("section", "ray", "dp"))
    attn_grad = lax.dot_general(
        cotangent, w_mix, (((1,), (1,)), ((), ())), preferred_element_type=jnp.float32
    )
    attn_grad = attn_grad.astype(jnp.bfloat16).reshape(ray_rows, HEADS, head_dim)
    prob_grad = jnp.einsum("rhd,lhd->hrl", attn_grad, values, preferred_element_type=jnp.float32)
    delta = jnp.sum(probs * prob_grad, -1, keepdims=True)
    score_grad = (probs * (prob_grad - delta) * scale).astype(jnp.bfloat16)
    count = latent.shape[0] * lax.axis_size("ray")
    key_grad = jnp.einsum(
        "hrl,rhd->lhd", score_grad, query, preferred_element_type=jnp.float32
    ).reshape(count, width)
    value_grad = jnp.einsum(
        "hrl,rhd->lhd", probs_low, attn_grad, preferred_element_type=jnp.float32
    ).reshape(count, width)
    stacked = jnp.stack([key_grad, value_grad], 1)
    pair_rows = lax.psum_scatter(
        stacked.astype(jnp.bfloat16), "ray", scatter_dimension=0, tiled=True
    )
    pair_sum = lax.psum(pair_rows, "section")
    latent_grad = latent_rows(pair_sum, w_pairs)
    return (handed[None, None], finished[None], features[None], latent_grad[None], out_grad)


def solution(mesh):
    return jax.shard_map(
        local,
        mesh=mesh,
        in_specs=(
            P("section", "dp", "ray", None),
            P("section", None),
            P("section", None, None, "ray"),
            P("section", "ray", None),
            P("section", None),
            P("section", None, "ray"),
            P("section", "ray", None),
            P("dp", "ray", None),
            P("dp", ("section", "ray"), None),
            P("section", None),
            P("section", None, None),
            P("section", None),
            P("dp", ("section", "ray"), None),
        ),
        out_specs=(
            P("section", "dp", "ray", None),
            P("dp", "ray", "section"),
            P("dp", ("section", "ray"), None),
            P("dp", "ray", None),
            P(),
        ),
        check_vma=False,
    )
```

profile of v0, /device:TPU:2, one launch (start us, length us, event | category | flops | bytes accessed | tf_op | source)
XLA Modules:
  0.0 928.3 jit_solution(4946242236666145838)
XLA Ops:
  8.1 1.1 convert_reduce_fusion.1
  9.2 1.2 fusion.73
  10.4 1.9 fusion.75
  12.3 0.0 reduce-scatter.6.cloned.1.call-start
  12.4 1.4 copy.44
  13.8 42.5 %all-gather.7.cloned.1.call-done = bf16[1024,1024]{1,0:T(8,128)(2,1)} async-done(((bf16[128,1024]{1,0:T(8,128)(2,1)}), bf16[1024,1024]{1,0:T(8,128)(2,1)}) %all-gather.7.cloned.1.call-update) | async-done | bytes 2097168 | tf_op jit(solution)/shard_map/all_gather | solution.py:89
  56.3 2.6 convolution_convert_fusion.3
  58.9 4.9 fusion.97
  63.7 4.3 fusion.48
  68.1 2.1 convolution_convert_fusion.2
  70.1 0.0 all-gather.11.cloned.1.call-start
  70.2 0.5 all-gather.11.cloned.1.call-update
  70.7 0.0 all-gather.15.cloned.1.call-start
  70.8 0.5 all-gather.15.cloned.1.call-update
  71.3 0.0 all-gather.17.cloned.1.call-start
  71.4 0.5 all-gather.17.cloned.1.call-update
  71.9 0.0 all-gather.9.cloned.1.call-start
  71.9 39.7 %reduce-scatter.6.cloned.1.call-done = bf16[128,1024]{1,0:T(8,128)(2,1)} async-done(((bf16[1024,1024]{1,0:T(8,128)(2,1)}), bf16[128,1024]{1,0:T(8,128)(2,1)}) %reduce-scatter.6.cloned.1.call-update) | async-done | bytes 262160 | tf_op jit(solution)/shard_map/reduce_scatter | solution.py:92
  111.7 1.1 convert_reduce_fusion
  112.8 0.2 fusion.70
  113.0 0.9 fusion.72
  114.0 0.0 all-gather.13.cloned.1.call-start
  114.0 18.6 %all-gather.11.cloned.1.call-done = bf16[1024,2,1024]{2,1,0:T(2,128)(2,1)} async-done(((bf16[64,2,1024]{2,1,0:T(2,128)(2,1)}), bf16[1024,2,1024]{2,1,0:T(2,128)(2,1)}) %all-gather.11.cloned.1.call-update) | async-done | bytes 4194320 | tf_op jit(solution)/shard_map/all_gather | solution.py:124
  132.7 11.1 %copy.47 = bf16[1024,2,1024]{0,2,1:T(8,128)(2,1)} copy(bf16[1024,2,1024]{2,1,0:T(2,128)(2,1)} %all-gather.11.cloned.1.call-done) | data formatting | bytes 8388608 | tf_op jit(solution)/shard_map/all_gather | solution.py:124
  143.8 4.6 convolution_convert_fusion
  148.5 0.0 reduce-scatter.8.cloned.1.call-start
  148.5 39.0 %all-gather.15.cloned.1.call-done = bf16[1024,1024]{1,0:T(8,128)(2,1)} async-done(((bf16[64,1024]{1,0:T(8,128)(2,1)}), bf16[1024,1024]{1,0:T(8,128)(2,1)}) %all-gather.15.cloned.1.call-update) | async-done | bytes 2097168 | tf_op jit(solution)/shard_map/all_gather | solution.py:123
  187.5 2.3 convolution_convert_fusion.5
  189.8 1.0 copy.49
  190.8 51.5 %all-gather.17.cloned.1.call-done = bf16[1024,1024]{1,0:T(8,128)(2,1)} async-done(((bf16[64,1024]{1,0:T(8,128)(2,1)}), bf16[1024,1024]{1,0:T(8,128)(2,1)}) %all-gather.17.cloned.1.call-update) | async-done | bytes 2097168 | tf_op jit(solution)/shard_map/all_gather | solution.py:125
  242.3 2.3 convolution_convert_fusion.4
  244.6 1.0 copy.51
  245.6 39.2 %all-gather.9.cloned.1.call-done = bf16[1024,1024]{1,0:T(8,128)(2,1)} async-done(((bf16[128,1024]{1,0:T(8,128)(2,1)}), bf16[1024,1024]{1,0:T(8,128)(2,1)}) %all-gather.9.cloned.1.call-update) | async-done | bytes 2097168 | tf_op jit(solution)/shard_map/all_gather | solution.py:101
  284.9 5.8 convolution_convert_fusion.1
  290.7 0.2 reduce-scatter.10.cloned.1.call-start
  290.9 66.2 %all-gather.13.cloned.1.call-done = bf16[1024,2048]{1,0:T(8,128)(2,1)} async-done(((bf16[128,2048]{1,0:T(8,128)(2,1)}), bf16[1024,2048]{1,0:T(8,128)(2,1)}) %all-gather.13.cloned.1.call-update) | async-done | bytes 4194320 | tf_op jit(solution)/shard_map/all_gather | solution.py:131
  357.2 4.0 fusion.96
  361.2 2.6 copy.50
  363.8 2.9 copy.48
  366.7 9.8 %fusion.98 = (f32[16,256]{1,0:T(8,128)S(1)}, f32[16,256,1024]{2,1,0:T(8,128)}) fusion(bf16[256,16,64]{0,2,1:T(8,128)(2,1)S(1)} %bitcast.149, bf16[1024,16,64]{0,2,1:T(8,128)(2,1)} %bitcast.144), kind=kOutput, calls=%fused_computation.110 | convolution fusion | flops 549454848 | bytes 19415040 | tf_op jit(solution)/shard_map/sub | solution.py:30
  376.5 8.1 fusion.99
  384.5 38.2 %fusion.38 = bf16[16,64,1024]{2,1,0:T(8,128)(2,1)} fusion(bf16[256,16,64]{0,2,1:T(8,128)(2,1)S(1)} %bitcast.150, f32[16,256,1024]{2,1,0:T(8,128)} %fusion.99, f32[16,256,1024]{2,1,0:T(8,128)} %get-tuple-element.18, f32[16,256]{1,0:T(8,128)S(1)} %get-tuple-element.17), kind=kOutput, calls=%fused_computation.40 | convolution fusion | flops 567284736 | bytes 36192256 | tf_op jit(solution)/shard_map/hrl,rhd->lhd/dot_general | solution.py:170
  422.8 7.1 fusion.35
  429.9 2.4 pad_maximum_fusion
  432.3 6.5 copy.57
  438.8 0.0 all-reduce.6.cloned.1.call-start
  438.9 1.9 broadcast_select_fusion
  440.8 52.2 %reduce-scatter.10.cloned.1.call-done = bf16[128,2048]{1,0:T(8,128)(2,1)} async-done(((bf16[1024,2048]{1,0:T(8,128)(2,1)}), bf16[128,2048]{1,0:T(8,128)(2,1)}) %reduce-scatter.10.cloned.1.call-update) | async-done | bytes 524304
  492.9 2.0 copy.58
  495.0 0.3 all-reduce.4.cloned.1.call-start
  495.3 8.5 fusion.42
  503.8 2.7 fusion.78
  506.5 10.0 %fusion.95 = (bf16[1024,1,1024]{2,1,0:T(2,128)(2,1)}, bf16[1024,1,1024]{2,1,0:T(2,128)(2,1)}) fusion(bf16[1024,2,1024]{2,1,0:T(2,128)(2,1)} %all-gather.11.cloned.1.call-done), kind=kLoop, calls=%fused_computation.107 | loop fusion | bytes 8388608 | tf_op jit(solution)/shard_map/slice | solution.py:49
  516.5 1.9 collective-permute-start
  518.5 1.5 fusion.45
  520.0 4.7 collective-permute-done
  524.7 109.9 %all-reduce.6.cloned.1.call-done = (bf16[128,1024]{1,0:T(8,128)(2,1)}, bf16[128,2,1024]{0,2,1:T(8,128)(2,1)}) async-done(((bf16[128,1024]{1,0:T(8,128)(2,1)}, bf16[128,2,1024]{0,2,1:T(8,128)(2,1)}), (bf16[128,1024]{1,0:T(8,128)(2,1)}, bf16[128,2,1024]{0,2,1:T(8,128)(2,1)})) %all-reduce.6.cloned.1.call-update) | async-done | bytes 786448 | tf_op jit(solution)/shard_map/psum | solution.py:18
  634.6 0.8 constant_dynamic-slice_fusion
  635.5 0.7 copy.46
  636.2 3.1 fusion.33
  639.3 3.9 fusion.49
  643.2 272.5 %all-reduce.4.cloned.1.call-done = f32[1024,1024]{1,0:T(8,128)} async-done(((f32[1024,1024]{1,0:T(8,128)}), f32[1024,1024]{1,0:T(8,128)}) %all-reduce.4.cloned.1.call-update) | async-done | bytes 4194320 | tf_op jit(solution)/shard_map/psum | solution.py:161
  915.7 0.7 copy.75
  916.4 4.8 copy.76
  (44 shorter events, 0.3 us)
Async XLA Ops:
  8.0 276.9 %copy-start = (bf16[1,512,1024]{2,1,0:T(8,128)(2,1)S(1)}, bf16[1,512,1024]{2,1,0:T(8,128)(2,1)}, u32[]{:S(2)}) copy-start(bf16[1,512,1024]{2,1,0:T(8,128)(2,1)} %param.19) | copy-start | bytes 3145732
  8.0 48.2 %all-gather.7.cloned.1.call-start = ((), (), s32[]{:S(2)}) async-start(), calls=%async_computation.3 | async-start | bytes 2359296 | tf_op jit(solution)/shard_map/all_gather | solution.py:89
  12.3 99.4 %reduce-scatter.6.cloned.1.call-start = ((), (), s32[]{:S(2)}) async-start(), calls=%async_computation.4 | async-start | bytes 2359296 | tf_op jit(solution)/shard_map/reduce_scatter | solution.py:92
  63.7 4.3 copy-start.11
  68.0 43.6 %copy-start.2 = (bf16[1,1,128,1024]{3,2,1,0:T(8,128)(2,1)S(1)}, bf16[1,1,128,1024]{3,2,1,0:T(8,128)(2,1)}, u32[]{:S(2)}) copy-start(bf16[1,1,128,1024]{3,2,1,0:T(8,128)(2,1)} %param.13) | copy-start | bytes 786436
  68.0 45.0 %copy-start.14 = (f32[1,1024]{1,0:T(1,128)S(1)}, f32[1,1024]{1,0:T(1,128)}, u32[]{:S(2)}) copy-start(f32[1,1024]{1,0:T(1,128)} %param.17) | copy-start | bytes 12292
  70.1 62.5 %all-gather.11.cloned.1.call-start = ((), (), s32[]{:S(2)}) async-start(), calls=%async_computation.7 | async-start | bytes 4456448 | tf_op jit(solution)/shard_map/all_gather | solution.py:124
  70.7 116.8 %all-gather.15.cloned.1.call-start = ((), (), s32[]{:S(2)}) async-start(), calls=%async_computation.9 | async-start | bytes 2228224 | tf_op jit(solution)/shard_map/all_gather | solution.py:123
  71.3 171.0 %all-gather.17.cloned.1.call-start = ((), (), s32[]{:S(2)}) async-start(), calls=%async_computation.10 | async-start | bytes 2228224 | tf_op jit(solution)/shard_map/all_gather | solution.py:125
  71.9 213.0 %all-gather.9.cloned.1.call-start = ((), (), s32[]{:S(2)}) async-start(), calls=%async_computation.5 | async-start | bytes 2359296 | tf_op jit(solution)/shard_map/all_gather | solution.py:101
  114.0 29.8 %copy-start.12 = (bf16[1,128,1024]{2,1,0:T(8,128)(2,1)S(1)}, bf16[1,128,1024]{2,1,0:T(8,128)(2,1)}, u32[]{:S(2)}) copy-start(bf16[1,128,1024]{2,1,0:T(8,128)(2,1)} %param.20) | copy-start | bytes 786436
  114.0 243.2 %all-gather.13.cloned.1.call-start = ((), (), s32[]{:S(2)}) async-start(), calls=%async_computation.8 | async-start | bytes 4718592 | tf_op jit(solution)/shard_map/all_gather | solution.py:131
  143.8 43.7 %copy-start.8 = (bf16[1,256,1024]{2,1,0:T(8,128)(2,1)S(1)}, bf16[1,256,1024]{2,1,0:T(8,128)(2,1)}, u32[]{:S(2)}) copy-start(bf16[1,256,1024]{2,1,0:T(8,128)(2,1)} %param.21) | copy-start | bytes 1572868
  143.8 98.5 %copy-start.6 = (bf16[1,256,1024]{2,1,0:T(8,128)(2,1)S(1)}, bf16[1,256,1024]{2,1,0:T(8,128)(2,1)}, u32[]{:S(2)}) copy-start(bf16[1,256,1024]{2,1,0:T(8,128)(2,1)} %param.25) | copy-start | bytes 1572868
  148.5 290.5 %reduce-scatter.8.cloned.1.call-start = ((), (), s32[]{:S(2)}) async-start(), calls=%async_computation.6 | async-start | bytes 2359296 | tf_op jit(solution)/shard_map/reduce_scatter | solution.py:109
  290.7 202.2 %reduce-scatter.10.cloned.1.call-start = ((), (), s32[]{:S(2)}) async-start(), calls=%async_computation.12 | async-start | bytes 4718592
  361.2 5.4 copy-start.10
  366.6 9.8 %copy-start.4 = (bf16[256,1024]{0,1:T(8,128)(2,1)S(1)}, bf16[256,1024]{0,1:T(8,128)(2,1)}, u32[]{:S(2)}) copy-start(bf16[256,1024]{0,1:T(8,128)(2,1)} %copy.51) | copy-start | bytes 1572868
  422.8 7.1 copy-start.5
  438.8 195.8 %all-reduce.6.cloned.1.call-start = ((), (), s32[]{:S(2)}) async-start(), calls=%async_computation.13 | async-start | bytes 1572864 | tf_op jit(solution)/shard_map/psum | solution.py:18
  495.0 8.8 copy-start.7
  495.0 420.7 %all-reduce.4.cloned.1.call-start = ((), (), s32[]{:S(2)}) async-start(), calls=%async_computation.11 | async-start | bytes 8388608 | tf_op jit(solution)/shard_map/psum | solution.py:161
  506.5 10.0 %copy-start.13 = (bf16[128,1024]{1,0:T(8,128)(2,1)S(1)}, bf16[128,1024]{1,0:T(8,128)(2,1)}, u32[]{:S(2)}) copy-start(bf16[128,1024]{1,0:T(8,128)(2,1)} %get-tuple-element.8) | copy-start | bytes 786436
  506.5 11.9 %copy-start.3 = (bf16[1024,1024]{1,0:T(8,128)(2,1)S(1)}, bf16[1024,1024]{1,0:T(8,128)(2,1)}, u32[]{:S(2)}) copy-start(bf16[1024,1024]{1,0:T(8,128)(2,1)} %all-gather.17.cloned.1.call-done) | copy-start | bytes 6291460
  506.5 11.9 %copy-start.9 = (bf16[1,256,1024]{2,1,0:T(8,128)(2,1)S(1)}, bf16[1,256,1024]{2,1,0:T(8,128)(2,1)}, u32[]{:S(2)}) copy-start(bf16[1,256,1024]{2,1,0:T(8,128)(2,1)} %param.21) | copy-start | bytes 1572868
  516.5 8.2 collective-permute-start
  915.7 5.5 copy-start.1
Sparse Core Ops, SparseCore 0:
  12.4 43.7 all-gather.6
  70.3 41.3 reduce-scatter.5
  290.8 69.1 reduce-scatter.7
  439.0 53.9 reduce-scatter.9
Sparse Core Ops, SparseCore 1:
  73.4 59.3 all-gather.10
  135.3 52.1 all-gather.14
  190.1 52.1 all-gather.16
  244.7 40.1 all-gather.8
  286.7 70.4 all-gather.12
  495.1 139.5 all-reduce.5
  640.0 275.7 all-reduce.3
where the time goes:
time: 929 us; the launch traced here: 928 us
  waiting for transfers between devices  738 us (79%)
  matrix products  112 us (12%)
  local copies, waits for them, and re-layouts  49.6 us (5%)
  between operations  15.6 us (2%)
  other arithmetic  10.7 us (1%)
    psum x1, waiting for transfers between devices, local(): out_grad = lax.psum(mix_term, ('section', 'ray', 'dp'))  273 us
    psum x1, waiting for transfers between devices, spread_2(): return lax.psum(jnp.where(mine, value, jnp.zeros_like(value)), axis)  110 us
    all_gather x1, waiting for transfers between devices, local(): lax.all_gather(jnp.dot(latent, flat_pairs, preferred_element_type=jnp.flo...  66.2 us
    unnamed x12, waiting for transfers between devices  53.9 us
    all_gather x1, waiting for transfers between devices, local(): lax.all_gather(dec_out, 'section', axis=0, tiled=True)  51.5 us
    all_gather x1, waiting for transfers between devices, local(): lax.all_gather(normed, 'ray', axis=0, tiled=True)  42.5 us
    reduce_scatter x1, waiting for transfers between devices, local(): lax.psum_scatter(jnp.dot(mixed, w_attn_out, preferred_element_type=jnp.fl...  39.7 us
    all_gather x1, waiting for transfers between devices, local(): lax.all_gather(layer_norm(hidden, gain_two).astype(jnp.bfloat16), 'ray',...  39.2 us
  transfers between devices with their start and end apart: 12, of which 11 were waited for; matrix products, arithmetic and copies ran while one was open for 16% of the time, Pallas kernels for 0%

commit v1 on v0

--- a/solution.py
+++ b/solution.py
@@ -122,7 +122,9 @@
     w_query, w_pairs, w_mix = (
         lax.all_gather(dec_query, "section", axis=0, tiled=True),
         lax.all_gather(dec_kv, "section", axis=0, tiled=True),
-        lax.all_gather(dec_out, "section", axis=0, tiled=True),
+        jnp.concatenate(
+            lax.all_to_all(jnp.stack([dec_out] * lax.axis_size("section")), "section", 0, 0), axis=0
+        ),
     )
     latent = set_latent[0]
     queries = ray_queries[0]

time: 929 us -> 881 us (0.948)
  waiting for transfers between devices: 738 us -> 658 us
  blocking collectives: 0 us -> 31.8 us
    all_gather x1 -> x0, waiting for transfers between devices: 51.5 us -> none  [local(): lax.all_gather(dec_out, 'section', axis=0, tiled=True)]
    all_to_all x0 -> x1, blocking collectives: none -> 31.8 us  [local(): lax.all_to_all(jnp.stack([dec_out] * lax.axis_size('section')), 'section'...]
    all_gather x1, waiting for transfers between devices: 39 us -> 10.6 us  [local(): lax.all_gather(dec_query, 'section', axis=0, tiled=True)]
    unnamed x12 -> x11, waiting for transfers between devices: 53.9 us -> 53.3 us
  transfers between devices with their start and end apart: 12 -> 11, of which waited for: 11 -> 10; matrix products, arithmetic and copies ran while one was open for 16% -> 16% of each run, Pallas kernels for 0% -> 0%
where the time goes in v1:
time: 881 us; the launch traced here: 880 us
  waiting for transfers between devices  658 us (75%)
  matrix products  110 us (12%)
  local copies, waits for them, and re-layouts  51.2 us (6%)
  blocking collectives  31.8 us (4%)
  between operations  15.6 us (2%)
  other arithmetic  10.7 us (1%)
    psum x1, waiting for transfers between devices, local(): out_grad = lax.psum(mix_term, ('section', 'ray', 'dp'))  273 us
    psum x1, waiting for transfers between devices, spread_2(): return lax.psum(jnp.where(mine, value, jnp.zeros_like(value)), axis)  110 us
    all_gather x1, waiting for transfers between devices, local(): lax.all_gather(jnp.dot(latent, flat_pairs, preferred_element_type=jnp.flo...  66.2 us
    unnamed x11, waiting for transfers between devices  53.3 us
    all_gather x1, waiting for transfers between devices, local(): lax.all_gather(normed, 'ray', axis=0, tiled=True)  42.5 us
    reduce_scatter x1, waiting for transfers between devices, local(): lax.psum_scatter(jnp.dot(mixed, w_attn_out, preferred_element_type=jnp.fl...  40.3 us
    all_gather x1, waiting for transfers between devices, local(): lax.all_gather(layer_norm(hidden, gain_two).astype(jnp.bfloat16), 'ray',...  39.4 us
    dot_general x1, matrix products, local(): jnp.einsum('hrl,rhd->lhd', score_grad, query, preferred_element_type=jnp....  38.2 us
  transfers between devices with their start and end apart: 11, of which 10 were waited for; matrix products, arithmetic and copies ran while one was open for 16% of the time, Pallas kernels for 0%

profile of v1, /device:TPU:2, one launch (start us, length us, event | category | flops | bytes accessed | tf_op | source)
XLA Modules:
  0.0 880.2 jit_solution(10256089633738596450)
XLA Ops:
  8.1 1.1 convert_reduce_fusion.1
  9.2 1.2 fusion.74
  10.4 1.9 fusion.76
  12.3 0.0 reduce-scatter.6.cloned.1.call-start
  12.4 1.4 copy.44
  13.8 42.5 %all-gather.6.cloned.1.call-done = bf16[1024,1024]{1,0:T(8,128)(2,1)} async-done(((bf16[128,1024]{1,0:T(8,128)(2,1)}), bf16[1024,1024]{1,0:T(8,128)(2,1)}) %all-gather.6.cloned.1.call-update) | async-done | bytes 2097168 | tf_op jit(solution)/shard_map/all_gather | solution.py:89
  56.3 2.6 convolution_convert_fusion.3
  58.9 4.9 fusion.99
  63.8 4.3 fusion.49
  68.1 2.1 convolution_convert_fusion.2
  70.1 0.0 all-gather.10.cloned.1.call-start
  70.2 0.5 all-gather.10.cloned.1.call-update
  70.7 0.0 all-gather.14.cloned.1.call-start
  70.8 0.5 all-gather.14.cloned.1.call-update
  71.3 0.0 all-gather.8.cloned.1.call-start
  71.4 40.3 %reduce-scatter.6.cloned.1.call-done = bf16[128,1024]{1,0:T(8,128)(2,1)} async-done(((bf16[1024,1024]{1,0:T(8,128)(2,1)}), bf16[128,1024]{1,0:T(8,128)(2,1)}) %reduce-scatter.6.cloned.1.call-update) | async-done | bytes 262160 | tf_op jit(solution)/shard_map/reduce_scatter | solution.py:92
  111.7 1.1 convert_reduce_fusion
  112.8 0.2 fusion.71
  113.1 0.9 fusion.73
  114.0 0.0 all-gather.12.cloned.1.call-start
  114.1 18.6 %all-gather.10.cloned.1.call-done = bf16[1024,2,1024]{2,1,0:T(2,128)(2,1)} async-done(((bf16[64,2,1024]{2,1,0:T(2,128)(2,1)}), bf16[1024,2,1024]{2,1,0:T(2,128)(2,1)}) %all-gather.10.cloned.1.call-update) | async-done | bytes 4194320 | tf_op jit(solution)/shard_map/all_gather | solution.py:124
  132.7 11.1 %copy.47 = bf16[1024,2,1024]{0,2,1:T(8,128)(2,1)} copy(bf16[1024,2,1024]{2,1,0:T(2,128)(2,1)} %all-gather.10.cloned.1.call-done) | data formatting | bytes 8388608 | tf_op jit(solution)/shard_map/all_gather | solution.py:124
  143.8 4.6 convolution_convert_fusion
  148.4 0.0 reduce-scatter.8.cloned.1.call-start
  148.5 0.3 stack.5
  148.7 31.8 %all_to_all.5 = bf16[16,64,1024]{2,1,0:T(8,128)(2,1)S(1)} all-to-all(bf16[16,64,1024]{2,1,0:T(8,128)(2,1)S(1)} %stack.5), channel_id=1, replica_groups=mesh['section'=16,'ray'=8,'dp'=2] {'section'}, dimensions={0} | all-to-all | bytes 4194304 | tf_op jit(solution)/shard_map/all_to_all | solution.py:126
  180.5 1.3 copy-done.2
  181.8 0.8 convolution_convert_fusion.4
  182.6 1.0 copy.51
  183.6 10.6 %all-gather.14.cloned.1.call-done = bf16[1024,1024]{1,0:T(8,128)(2,1)} async-done(((bf16[64,1024]{1,0:T(8,128)(2,1)}), bf16[1024,1024]{1,0:T(8,128)(2,1)}) %all-gather.14.cloned.1.call-update) | async-done | bytes 2097168 | tf_op jit(solution)/shard_map/all_gather | solution.py:123
  194.2 2.3 convolution_convert_fusion.5
  196.5 1.0 copy.49
  197.5 39.4 %all-gather.8.cloned.1.call-done = bf16[1024,1024]{1,0:T(8,128)(2,1)} async-done(((bf16[128,1024]{1,0:T(8,128)(2,1)}), bf16[1024,1024]{1,0:T(8,128)(2,1)}) %all-gather.8.cloned.1.call-update) | async-done | bytes 2097168 | tf_op jit(solution)/shard_map/all_gather | solution.py:101
  236.9 5.8 convolution_convert_fusion.1
  242.7 0.2 reduce-scatter.10.cloned.1.call-start
  242.9 66.2 %all-gather.12.cloned.1.call-done = bf16[1024,2048]{1,0:T(8,128)(2,1)} async-done(((bf16[128,2048]{1,0:T(8,128)(2,1)}), bf16[1024,2048]{1,0:T(8,128)(2,1)}) %all-gather.12.cloned.1.call-update) | async-done | bytes 4194320 | tf_op jit(solution)/shard_map/all_gather | solution.py:133
  309.2 4.0 fusion.98
  313.2 2.6 copy.50
  315.8 2.9 copy.48
  318.6 9.8 %fusion.100 = (f32[16,256]{1,0:T(8,128)S(1)}, f32[16,256,1024]{2,1,0:T(8,128)}) fusion(bf16[256,16,64]{0,2,1:T(8,128)(2,1)S(1)} %bitcast.159, bf16[1024,16,64]{0,2,1:T(8,128)(2,1)} %bitcast.154), kind=kOutput, calls=%fused_computation.112 | convolution fusion | flops 549454848 | bytes 19415040 | tf_op jit(solution)/shard_map/sub | solution.py:30
  328.5 8.1 fusion.101
  336.6 38.2 %fusion.38 = bf16[16,64,1024]{2,1,0:T(8,128)(2,1)} fusion(bf16[256,16,64]{0,2,1:T(8,128)(2,1)S(1)} %bitcast.160, f32[16,256,1024]{2,1,0:T(8,128)} %fusion.101, f32[16,256,1024]{2,1,0:T(8,128)} %get-tuple-element.18, f32[16,256]{1,0:T(8,128)S(1)} %get-tuple-element.17), kind=kOutput, calls=%fused_computation.40 | convolution fusion | flops 567284736 | bytes 36192256 | tf_op jit(solution)/shard_map/hrl,rhd->lhd/dot_general | solution.py:172
  374.7 7.1 fusion.35
  381.9 2.4 pad_maximum_fusion
  384.2 6.5 copy.57
  390.8 0.0 all-reduce.6.cloned.1.call-start
  390.9 1.9 broadcast_select_fusion
  392.7 52.1 %reduce-scatter.10.cloned.1.call-done = bf16[128,2048]{1,0:T(8,128)(2,1)} async-done(((bf16[1024,2048]{1,0:T(8,128)(2,1)}), bf16[128,2048]{1,0:T(8,128)(2,1)}) %reduce-scatter.10.cloned.1.call-update) | async-done | bytes 524304
  444.9 2.1 copy.58
  447.0 0.3 all-reduce.4.cloned.1.call-start
  447.2 8.5 fusion.43
  455.7 2.7 fusion.79
  458.5 10.0 %fusion.97 = (bf16[1024,1,1024]{2,1,0:T(2,128)(2,1)}, bf16[1024,1,1024]{2,1,0:T(2,128)(2,1)}) fusion(bf16[1024,2,1024]{2,1,0:T(2,128)(2,1)} %all-gather.10.cloned.1.call-done), kind=kLoop, calls=%fused_computation.109 | loop fusion | bytes 8388608 | tf_op jit(solution)/shard_map/slice | solution.py:49
  468.5 1.9 collective-permute-start
  470.4 1.5 fusion.46
  472.0 4.7 collective-permute-done
  476.7 109.7 %all-reduce.6.cloned.1.call-done = (bf16[128,1024]{1,0:T(8,128)(2,1)}, bf16[128,2,1024]{0,2,1:T(8,128)(2,1)}) async-done(((bf16[128,1024]{1,0:T(8,128)(2,1)}, bf16[128,2,1024]{0,2,1:T(8,128)(2,1)}), (bf16[128,1024]{1,0:T(8,128)(2,1)}, bf16[128,2,1024]{0,2,1:T(8,128)(2,1)})) %all-reduce.6.cloned.1.call-update) | async-done | bytes 786448 | tf_op jit(solution)/shard_map/psum | solution.py:18
  586.4 0.8 constant_dynamic-slice_fusion
  587.2 0.7 copy.46
  587.9 3.1 fusion.33
  591.1 3.9 fusion.50
  594.9 272.7 %all-reduce.4.cloned.1.call-done = f32[1024,1024]{1,0:T(8,128)} async-done(((f32[1024,1024]{1,0:T(8,128)}), f32[1024,1024]{1,0:T(8,128)}) %all-reduce.4.cloned.1.call-update) | async-done | bytes 4194320 | tf_op jit(solution)/shard_map/psum | solution.py:163
  867.6 0.7 copy.75
  868.3 4.8 copy.76
  (47 shorter events, 0.3 us)
Async XLA Ops:
  8.0 228.9 %copy-start = (bf16[1,512,1024]{2,1,0:T(8,128)(2,1)S(1)}, bf16[1,512,1024]{2,1,0:T(8,128)(2,1)}, u32[]{:S(2)}) copy-start(bf16[1,512,1024]{2,1,0:T(8,128)(2,1)} %param.19) | copy-start | bytes 3145732
  8.0 48.2 %all-gather.6.cloned.1.call-start = ((), (), s32[]{:S(2)}) async-start(), calls=%async_computation.4 | async-start | bytes 2359296 | tf_op jit(solution)/shard_map/all_gather | solution.py:89
  12.3 99.4 %reduce-scatter.6.cloned.1.call-start = ((), (), s32[]{:S(2)}) async-start(), calls=%async_computation.5 | async-start | bytes 2359296 | tf_op jit(solution)/shard_map/reduce_scatter | solution.py:92
  63.7 4.3 copy-start.12
  68.0 43.7 %copy-start.4 = (bf16[1,1,128,1024]{3,2,1,0:T(8,128)(2,1)S(1)}, bf16[1,1,128,1024]{3,2,1,0:T(8,128)(2,1)}, u32[]{:S(2)}) copy-start(bf16[1,1,128,1024]{3,2,1,0:T(8,128)(2,1)} %param.13) | copy-start | bytes 786436
  68.0 45.0 %copy-start.16 = (f32[1,1024]{1,0:T(1,128)S(1)}, f32[1,1024]{1,0:T(1,128)}, u32[]{:S(2)}) copy-start(f32[1,1024]{1,0:T(1,128)} %param.17) | copy-start | bytes 12292
  70.1 62.5 %all-gather.10.cloned.1.call-start = ((), (), s32[]{:S(2)}) async-start(), calls=%async_computation.8 | async-start | bytes 4456448 | tf_op jit(solution)/shard_map/all_gather | solution.py:124
  70.7 123.4 %all-gather.14.cloned.1.call-start = ((), (), s32[]{:S(2)}) async-start(), calls=%async_computation.10 | async-start | bytes 2228224 | tf_op jit(solution)/shard_map/all_gather | solution.py:123
  71.3 165.6 %all-gather.8.cloned.1.call-start = ((), (), s32[]{:S(2)}) async-start(), calls=%async_computation.6 | async-start | bytes 2359296 | tf_op jit(solution)/shard_map/all_gather | solution.py:101
  114.0 29.8 %copy-start.13 = (bf16[1,128,1024]{2,1,0:T(8,128)(2,1)S(1)}, bf16[1,128,1024]{2,1,0:T(8,128)(2,1)}, u32[]{:S(2)}) copy-start(bf16[1,128,1024]{2,1,0:T(8,128)(2,1)} %param.20) | copy-start | bytes 786436
  114.0 195.2 %all-gather.12.cloned.1.call-start = ((), (), s32[]{:S(2)}) async-start(), calls=%async_computation.9 | async-start | bytes 4718592 | tf_op jit(solution)/shard_map/all_gather | solution.py:133
  143.8 4.6 copy-start.15
  148.4 33.4 %copy-start.7 = (bf16[1,256,1024]{2,1,0:T(8,128)(2,1)S(1)}, bf16[1,256,1024]{2,1,0:T(8,128)(2,1)}, u32[]{:S(2)}) copy-start(bf16[1,256,1024]{2,1,0:T(8,128)(2,1)} %param.25) | copy-start | bytes 1572868
  148.4 242.5 %reduce-scatter.8.cloned.1.call-start = ((), (), s32[]{:S(2)}) async-start(), calls=%async_computation.7 | async-start | bytes 2359296 | tf_op jit(solution)/shard_map/reduce_scatter | solution.py:109
  148.7 45.4 %copy-start.9 = (bf16[1,256,1024]{2,1,0:T(8,128)(2,1)S(1)}, bf16[1,256,1024]{2,1,0:T(8,128)(2,1)}, u32[]{:S(2)}) copy-start(bf16[1,256,1024]{2,1,0:T(8,128)(2,1)} %param.21) | copy-start | bytes 1572868
  180.5 1.3 copy-start.2
  242.7 202.2 %reduce-scatter.10.cloned.1.call-start = ((), (), s32[]{:S(2)}) async-start(), calls=%async_computation.12 | async-start | bytes 4718592
  313.2 5.4 copy-start.11
  318.6 9.8 %copy-start.5 = (bf16[256,1024]{0,1:T(8,128)(2,1)S(1)}, bf16[256,1024]{0,1:T(8,128)(2,1)}, u32[]{:S(2)}) copy-start(bf16[256,1024]{0,1:T(8,128)(2,1)} %copy.51) | copy-start | bytes 1572868
  374.7 7.1 copy-start.6
  390.8 195.6 %all-reduce.6.cloned.1.call-start = ((), (), s32[]{:S(2)}) async-start(), calls=%async_computation.13 | async-start | bytes 1572864 | tf_op jit(solution)/shard_map/psum | solution.py:18
  446.9 8.8 copy-start.8
  447.0 420.6 %all-reduce.4.cloned.1.call-start = ((), (), s32[]{:S(2)}) async-start(), calls=%async_computation.11 | async-start | bytes 8388608 | tf_op jit(solution)/shard_map/psum | solution.py:163
  458.4 10.0 %copy-start.14 = (bf16[128,1024]{1,0:T(8,128)(2,1)S(1)}, bf16[128,1024]{1,0:T(8,128)(2,1)}, u32[]{:S(2)}) copy-start(bf16[128,1024]{1,0:T(8,128)(2,1)} %get-tuple-element.8) | copy-start | bytes 786436
  458.5 11.9 %copy-start.3 = (bf16[16,64,1024]{2,1,0:T(8,128)(2,1)S(1)}, bf16[16,64,1024]{2,1,0:T(8,128)(2,1)}, u32[]{:S(2)}) copy-start(bf16[16,64,1024]{2,1,0:T(8,128)(2,1)} %copy-done.2) | copy-start | bytes 6291460
  458.5 11.9 %copy-start.10 = (bf16[1,256,1024]{2,1,0:T(8,128)(2,1)S(1)}, bf16[1,256,1024]{2,1,0:T(8,128)(2,1)}, u32[]{:S(2)}) copy-start(bf16[1,256,1024]{2,1,0:T(8,128)(2,1)} %param.21) | copy-start | bytes 1572868
  468.5 8.2 collective-permute-start
  867.6 5.5 copy-start.1
Sparse Core Ops, SparseCore 0:
  12.4 43.7 all-gather.5
  70.3 41.3 reduce-scatter.5
  242.8 69.1 reduce-scatter.7
  390.9 53.8 reduce-scatter.9
Sparse Core Ops, SparseCore 1:
  73.4 59.3 all-gather.9
  135.3 58.8 all-gather.13
  196.4 40.4 all-gather.7
  238.7 70.4 all-gather.11
  447.0 139.3 all-reduce.5
  591.9 275.7 all-reduce.3
